TPU v7x, 32 devices: a whole 2x2x4 slice. The times are simulated.
32 devices in a mesh: dom: 16 (over z, y, x), ens: 2 (over core).
Axes of the slice: x: 2, y: 2, z: 4, core: 2. Of those that a mesh axis runs over, the one named last changes fastest.
Arguments:
- alpha: float32 [20, 4, 128, 512], P('ens', None, 'dom'), may hold values from -2.5 to 2.5
- perturb: bfloat16 [20, 4, 128, 512], P('ens', None, 'dom'), may hold values from -6 to 6
- static_ctl: float32 [4, 128, 512], P(None, 'dom'), may hold values from -6 to 6
- sigma: float32 [4, 128, 512], P(None, 'dom'), may hold values from 0.3 to 3
- class_index: int32 [4, 128, 512], P(None, 'dom'), may hold values from 0 to 7
- class_kappa: float32 [8], replicated, may hold values from 0.02 to 0.24
- obs_cell: int32 [32768], P('dom'), may hold values from 0 to 16383
- obs_value: float32 [32768], P('dom'), may hold values from -6 to 6
- obs_weight: float32 [32768], P('dom'), may hold values from 2 to 20
Outputs:
- grad_alpha: float32 [20, 4, 128, 512], P('ens', None, 'dom')
- grad_static: float32 [4, 128, 512], P(None, 'dom')
Inputs may be any that keep to these rules, and one draw needn't show every extreme that they name: obs_cell[k] is a cell, in the order level, column, row, of the block of 8 columns that starts at column (k // 2048) * 8.
All inputs are finite; a program needn't handle non-finite values.
Results may differ from a plain program's by a relative error of at most 0.0005.
Values sent between devices are 32-bit elements; how exact they have to be, the bound alone decides.
A program may use at most 64 MiB of HBM per device.

v0:
```python
import math

import jax
import jax.numpy as jnp
from jax import lax
from jax.sharding import PartitionSpec as P

PASSES = 4


def padded_2(block, sides, width):
    for axis, dim in sides:
        count = lax.axis_size(axis)
        forward = [(i, i + 1) for i in range(count - 1)]
        forward.append((count - 1, 0))
        backward = [(target, source) for source, target in forward]
        low = lax.ppermute(
            lax.slice_in_dim(block, block.shape[dim] - width, None, axis=dim), axis, forward
        )
        high = lax.ppermute(lax.slice_in_dim(block, 0, width, axis=dim), axis, backward)
        block = jnp.concatenate([low, block, high], axis=dim)
    return block


def lookup(class_index, class_kappa):
    coeff = jnp.zeros(class_index.shape, jnp.float32)
    for number in range(class_kappa.shape[0]):
        coeff = jnp.where(class_index == number, class_kappa[number], coeff)
    return coeff


def one_pass(field, coeff):
    face_x = 0.5 * (coeff[:, :-1] + coeff[:, 1:])
    flux_x = face_x * (field[..., 1:, :] - field[..., :-1, :])
    inner = field[..., 1:-1, :]
    inner_coeff = coeff[:, 1:-1]
    face_y = 0.5 * (inner_coeff[..., :-1] + inner_coeff[..., 1:])
    flux_y = face_y * (inner[..., 1:] - inner[..., :-1])
    padded = jnp.pad(flux_y, [(0, 0)] * (flux_y.ndim - 1) + [(1, 1)])
    return inner + (flux_x[..., 1:, :] - flux_x[..., :-1, :]) + (padded[..., 1:] - padded[..., :-1])


def diffuse(field, coeff_ext):
    extent = coeff_ext.shape[1]
    for index in range(PASSES):
        wide = padded_2(field, (("dom", 2),), 1)
        field = one_pass(wide, coeff_ext[:, PASSES - 1 : extent - PASSES + 1])
    return field


def per_device(
    alpha, perturb, static_ctl, sigma, class_index, class_kappa, obs_cell, obs_value, obs_weight
):
    coeff = lookup(class_index, class_kappa)
    coeff_ext = padded_2(coeff, (("dom", 1),), PASSES)
    members = alpha.shape[0] * lax.axis_size("ens")
    scale = 1.0 / math.sqrt(members - 1)
    smooth = diffuse(alpha, coeff_ext)
    partial_value = jnp.sum(perturb.astype(jnp.float32) * smooth, axis=0)
    local_vals = partial_value.reshape(-1)[obs_cell]
    summed = lax.psum(local_vals, "ens")
    values = (sigma * static_ctl).reshape(-1)[obs_cell] + scale * summed
    weighted = obs_weight * (values - obs_value)
    adjoint = (
        jnp.zeros((partial_value.size,), jnp.float32)
        .at[obs_cell]
        .add(weighted)
        .reshape(partial_value.shape)
    )
    grad_static = static_ctl + sigma * adjoint
    grad_alpha = alpha + scale * diffuse(perturb.astype(jnp.float32) * adjoint, coeff_ext)
    return (grad_alpha, grad_static)


def solution(mesh):
    return jax.shard_map(
        per_device,
        mesh=mesh,
        in_specs=(
            P("ens", None, "dom", None),
            P("ens", None, "dom", None),
            P(None, "dom", None),
            P(None, "dom", None),
            P(None, "dom", None),
            P(),
            P("dom"),
            P("dom"),
            P("dom"),
        ),
        out_specs=(P("ens", None, "dom", None), P(None, "dom", None)),
        check_vma=False,
    )
```

profile of v0, /device:TPU:0, one launch (start us, length us, event | category | flops | bytes accessed | tf_op | source)
XLA Modules:
  0.0 136.8 jit_solution(10196931838127274427)
XLA Ops:
  0.6 1.6 %fusion.57 = (f32[1]{0:T(128)}, f32[1]{0:T(128)}, f32[1]{0:T(128)}, f32[1]{0:T(128)}, f32[1]{0:T(128)}, /*index=5*/f32[1]{0:T(128)}, f32[1]{0:T(128)}, f32[1]{0:T(128)}) fusion(f32[8]{0:T(128)} %param.14), kind=kLoop, calls=%fused_computation.111 | loop fusion | bytes 64 | tf_op jit(solution)/shard_map/slice | solution.py:28
  2.3 6.0 %select_select_fusion = f32[4,8,512]{2,1,0:T(8,128)S(1)} fusion(s32[4,8,512]{2,1,0:T(8,128)} %param.13, f32[]{:T(128)} %bitcast.7, f32[]{:T(128)} %bitcast.6, f32[]{:T(128)} %bitcast.5, f32[]{:T(128)} %bitcast.4, f32[]{:T(128)} %bitcast.3, f32[]{:T(128)} %bitcast.2, f32[]{:T(128)} %bitcast.1, f32[]{:T(128)} %bitcast), kind=kLoop, calls=%fused_computation.95 | loop fusion | flops 262144 | bytes 131104 | tf_op jit(solution)/shard_map/jit(_where)/select_n | solution.py:28
  8.3 3.0 %collective-permute-start = (f32[4,4,512]{2,1,0:T(4,128)S(1)}, f32[4,4,512]{2,1,0:T(4,128)S(1)}, u32[]{:S(2)}, u32[]{:S(2)}) collective-permute-start(f32[4,4,512]{2,1,0:T(4,128)S(1)} %get-tuple-element.20), channel_id=1, source_target_pairs={{0,2},{2,4},{4,6},{6,8},{8,10},{10,12},{12,14},{14,16},{16,18},{18... | collective-permute-start | bytes 98312 | tf_op jit(solution)/shard_map/ppermute | solution.py:17
  11.3 4.1 %collective-permute-start.1 = (f32[4,4,512]{2,1,0:T(4,128)S(1)}, f32[4,4,512]{2,1,0:T(4,128)S(1)}, u32[]{:S(2)}, u32[]{:S(2)}) collective-permute-start(f32[4,4,512]{2,1,0:T(4,128)S(1)} %get-tuple-element.21), channel_id=1, source_target_pairs={{2,0},{4,2},{6,4},{8,6},{10,8},{12,10},{14,12},{16,14},{18,16},{20... | collective-permute-start | bytes 98312 | tf_op jit(solution)/shard_map/ppermute | solution.py:20
  15.4 1.5 %copy.19 = f32[10,4,8,512]{3,0,2,1:T(8,128)S(1)} copy(f32[10,4,8,512]{3,2,1,0:T(8,128)} %param.9) | data formatting | bytes 1310720 | tf_op args[0]
  17.5 2.0 %collective-permute-start.2 = (f32[10,4,1,512]{3,0,2,1:T(8,128)}, f32[10,4,1,512]{3,0,2,1:T(8,128)S(1)}, u32[]{:S(2)}, u32[]{:S(2)}) collective-permute-start(f32[10,4,1,512]{3,0,2,1:T(8,128)} %get-tuple-element.19), channel_id=1, source_target_pairs={{2,0},{4,2},{6,4},{8,6},{10,8},{12,10},{14,12},{16,14},{18,16},{20... | collective-permute-start | bytes 245768 | tf_op jit(solution)/shard_map/ppermute | solution.py:20
  21.2 11.8 %gather_fusion = f32[2048]{0:T(1024)S(1)} fusion(f32[16384]{0:T(1024)S(1)} %bitcast.14, s32[2048]{0:T(1024)S(1)} %get-tuple-element.22), kind=kCustom, calls=%fused_computation | custom fusion | bytes 24576 | tf_op jit(solution)/shard_map/gather | solution.py:62
  35.0 5.6 %collective-permute-start.4 = (f32[10,4,1,512]{3,0,2,1:T(8,128)S(1)}, f32[10,4,1,512]{3,0,2,1:T(8,128)S(1)}, u32[]{:S(2)}, u32[]{:S(2)}) collective-permute-start(f32[10,4,1,512]{3,0,2,1:T(8,128)S(1)} %get-tuple-element.17), channel_id=1, source_target_pairs={{2,0},{4,2},{6,4},{8,6},{10,8},{12,10},{14,12},{16,14},{18,16},{20... | collective-permute-start | bytes 245768 | tf_op jit(solution)/shard_map/ppermute | solution.py:20
  41.0 2.2 %collective-permute-done.4 = f32[10,4,1,512]{3,0,2,1:T(8,128)S(1)} collective-permute-done((f32[10,4,1,512]{3,0,2,1:T(8,128)S(1)}, f32[10,4,1,512]{3,0,2,1:T(8,128)S(1)}, u32[]{:S(2)}, u32[]{:S(2)}) %collective-permute-start.4) | collective-permute-done | bytes 81952 | tf_op jit(solution)/shard_map/ppermute | solution.py:20
  43.2 6.2 %collective-permute-done.5 = f32[10,4,1,512]{3,0,2,1:T(8,128)S(1)} collective-permute-done((f32[10,4,1,512]{3,0,2,1:T(8,128)S(1)}, f32[10,4,1,512]{3,0,2,1:T(8,128)S(1)}, u32[]{:S(2)}, u32[]{:S(2)}) %collective-permute-start.5) | collective-permute-done | bytes 81952 | tf_op jit(solution)/shard_map/ppermute | solution.py:17
  50.2 2.0 %collective-permute-start.7 = (f32[10,4,1,512]{3,0,2,1:T(8,128)S(1)}, f32[10,4,1,512]{3,0,2,1:T(8,128)S(1)}, u32[]{:S(2)}, u32[]{:S(2)}) collective-permute-start(f32[10,4,1,512]{3,0,2,1:T(8,128)S(1)} %get-tuple-element.14), channel_id=1, source_target_pairs={{0,2},{2,4},{4,6},{6,8},{8,10},{10,12},{12,14},{14,16},{16,18},{18... | collective-permute-start | bytes 245768 | tf_op jit(solution)/shard_map/ppermute | solution.py:17
  52.6 2.6 %collective-permute-done.6 = f32[10,4,1,512]{3,0,2,1:T(8,128)S(1)} collective-permute-done((f32[10,4,1,512]{3,0,2,1:T(8,128)S(1)}, f32[10,4,1,512]{3,0,2,1:T(8,128)S(1)}, u32[]{:S(2)}, u32[]{:S(2)}) %collective-permute-start.6) | collective-permute-done | bytes 81952 | tf_op jit(solution)/shard_map/ppermute | solution.py:20
  55.1 3.8 %collective-permute-done.7 = f32[10,4,1,512]{3,0,2,1:T(8,128)S(1)} collective-permute-done((f32[10,4,1,512]{3,0,2,1:T(8,128)S(1)}, f32[10,4,1,512]{3,0,2,1:T(8,128)S(1)}, u32[]{:S(2)}, u32[]{:S(2)}) %collective-permute-start.7) | collective-permute-done | bytes 81952 | tf_op jit(solution)/shard_map/ppermute | solution.py:17
  59.8 2.0 %collective-permute-start.9 = (f32[10,4,1,512]{3,0,2,1:T(8,128)S(1)}, f32[10,4,1,512]{3,0,2,1:T(8,128)S(1)}, u32[]{:S(2)}, u32[]{:S(2)}) collective-permute-start(f32[10,4,1,512]{3,0,2,1:T(8,128)S(1)} %get-tuple-element.12), channel_id=1, source_target_pairs={{0,2},{2,4},{4,6},{6,8},{8,10},{10,12},{12,14},{14,16},{16,18},{18... | collective-permute-start | bytes 245768 | tf_op jit(solution)/shard_map/ppermute | solution.py:17
  62.2 2.6 %collective-permute-done.8 = f32[10,4,1,512]{3,0,2,1:T(8,128)S(1)} collective-permute-done((f32[10,4,1,512]{3,0,2,1:T(8,128)S(1)}, f32[10,4,1,512]{3,0,2,1:T(8,128)S(1)}, u32[]{:S(2)}, u32[]{:S(2)}) %collective-permute-start.8) | collective-permute-done | bytes 81952 | tf_op jit(solution)/shard_map/ppermute | solution.py:20
  64.8 3.7 %collective-permute-done.9 = f32[10,4,1,512]{3,0,2,1:T(8,128)S(1)} collective-permute-done((f32[10,4,1,512]{3,0,2,1:T(8,128)S(1)}, f32[10,4,1,512]{3,0,2,1:T(8,128)S(1)}, u32[]{:S(2)}, u32[]{:S(2)}) %collective-permute-start.9) | collective-permute-done | bytes 81952 | tf_op jit(solution)/shard_map/ppermute | solution.py:17
  69.5 11.8 %gather_fusion.1 = f32[2048]{0:T(1024)S(1)} fusion(f32[16384]{0:T(1024)S(1)} %bitcast.13, s32[2048]{0:T(1024)S(1)} %get-tuple-element.22), kind=kCustom, calls=%fused_computation.1 | custom fusion | bytes 24576 | tf_op jit(solution)/shard_map/gather | solution.py:60
  81.3 2.5 %psum.7 = f32[2048]{0:T(1024)S(1)} all-reduce(f32[2048]{0:T(1024)S(1)} %gather_fusion.1), channel_id=1, replica_groups=mesh['dom'=16,'ens'=2] {'ens'}, use_global_device_ids=true, to_apply=%region_1.2 | all-reduce | flops 2048 | bytes 16384 | tf_op jit(solution)/shard_map/psum | solution.py:61
  83.9 11.4 %scatter_custom_fusion = f32[16384]{0:T(1024)S(1)} fusion(s32[2048]{0:T(1024)} %get-tuple-element.23, f32[2048]{0:T(1024)S(1)} %subtract_multiply_fusion, f32[]{:T(128)} %constant.12.clone.1), kind=kCustom, calls=%fused_computation.97 | custom fusion | flops 2048 | bytes 66048 | tf_op jit(solution)/shard_map/scatter-add | solution.py:67
  96.0 2.0 %collective-permute-start.11 = (f32[10,4,1,512]{3,0,2,1:T(8,128)S(1)}, f32[10,4,1,512]{3,0,2,1:T(8,128)S(1)}, u32[]{:S(2)}, u32[]{:S(2)}) collective-permute-start(f32[10,4,1,512]{3,0,2,1:T(8,128)S(1)} %get-tuple-element.10), channel_id=1, source_target_pairs={{0,2},{2,4},{4,6},{6,8},{8,10},{10,12},{12,14},{14,16},{16,18},{18... | collective-permute-start | bytes 245768 | tf_op jit(solution)/shard_map/ppermute | solution.py:17
  98.7 3.7 %collective-permute-done.10 = f32[10,4,1,512]{3,0,2,1:T(8,128)S(1)} collective-permute-done((f32[10,4,1,512]{3,0,2,1:T(8,128)S(1)}, f32[10,4,1,512]{3,0,2,1:T(8,128)S(1)}, u32[]{:S(2)}, u32[]{:S(2)}) %collective-permute-start.10) | collective-permute-done | bytes 81952 | tf_op jit(solution)/shard_map/ppermute | solution.py:20
  102.3 2.9 %collective-permute-done.11 = f32[10,4,1,512]{3,0,2,1:T(8,128)S(1)} collective-permute-done((f32[10,4,1,512]{3,0,2,1:T(8,128)S(1)}, f32[10,4,1,512]{3,0,2,1:T(8,128)S(1)}, u32[]{:S(2)}, u32[]{:S(2)}) %collective-permute-start.11) | collective-permute-done | bytes 81952 | tf_op jit(solution)/shard_map/ppermute | solution.py:17
  106.5 1.7 %collective-permute-start.13 = (f32[10,4,1,512]{3,0,2,1:T(8,128)S(1)}, f32[10,4,1,512]{3,0,2,1:T(8,128)S(1)}, u32[]{:S(2)}, u32[]{:S(2)}) collective-permute-start(f32[10,4,1,512]{3,0,2,1:T(8,128)S(1)} %get-tuple-element.8), channel_id=1, source_target_pairs={{0,2},{2,4},{4,6},{6,8},{8,10},{10,12},{12,14},{14,16},{16,18},{18... | collective-permute-start | bytes 245768 | tf_op jit(solution)/shard_map/ppermute | solution.py:17
  108.5 3.8 %collective-permute-done.12 = f32[10,4,1,512]{3,0,2,1:T(8,128)S(1)} collective-permute-done((f32[10,4,1,512]{3,0,2,1:T(8,128)S(1)}, f32[10,4,1,512]{3,0,2,1:T(8,128)S(1)}, u32[]{:S(2)}, u32[]{:S(2)}) %collective-permute-start.12) | collective-permute-done | bytes 81952 | tf_op jit(solution)/shard_map/ppermute | solution.py:20
  112.3 2.8 %collective-permute-done.13 = f32[10,4,1,512]{3,0,2,1:T(8,128)S(1)} collective-permute-done((f32[10,4,1,512]{3,0,2,1:T(8,128)S(1)}, f32[10,4,1,512]{3,0,2,1:T(8,128)S(1)}, u32[]{:S(2)}, u32[]{:S(2)}) %collective-permute-start.13) | collective-permute-done | bytes 81952 | tf_op jit(solution)/shard_map/ppermute | solution.py:17
  116.2 1.9 %collective-permute-start.15 = (f32[10,4,1,512]{3,0,2,1:T(8,128)S(1)}, f32[10,4,1,512]{3,0,2,1:T(8,128)S(1)}, u32[]{:S(2)}, u32[]{:S(2)}) collective-permute-start(f32[10,4,1,512]{3,0,2,1:T(8,128)S(1)} %get-tuple-element.6), channel_id=1, source_target_pairs={{0,2},{2,4},{4,6},{6,8},{8,10},{10,12},{12,14},{14,16},{16,18},{18... | collective-permute-start | bytes 245768 | tf_op jit(solution)/shard_map/ppermute | solution.py:17
  118.5 2.6 %collective-permute-done.14 = f32[10,4,1,512]{3,0,2,1:T(8,128)S(1)} collective-permute-done((f32[10,4,1,512]{3,0,2,1:T(8,128)S(1)}, f32[10,4,1,512]{3,0,2,1:T(8,128)S(1)}, u32[]{:S(2)}, u32[]{:S(2)}) %collective-permute-start.14) | collective-permute-done | bytes 81952 | tf_op jit(solution)/shard_map/ppermute | solution.py:20
  121.0 3.8 %collective-permute-done.15 = f32[10,4,1,512]{3,0,2,1:T(8,128)S(1)} collective-permute-done((f32[10,4,1,512]{3,0,2,1:T(8,128)S(1)}, f32[10,4,1,512]{3,0,2,1:T(8,128)S(1)}, u32[]{:S(2)}, u32[]{:S(2)}) %collective-permute-start.15) | collective-permute-done | bytes 81952 | tf_op jit(solution)/shard_map/ppermute | solution.py:17
  125.7 2.0 %collective-permute-start.17 = (f32[10,4,1,512]{3,0,2,1:T(8,128)S(1)}, f32[10,4,1,512]{3,0,2,1:T(8,128)S(1)}, u32[]{:S(2)}, u32[]{:S(2)}) collective-permute-start(f32[10,4,1,512]{3,0,2,1:T(8,128)S(1)} %get-tuple-element.4), channel_id=1, source_target_pairs={{0,2},{2,4},{4,6},{6,8},{8,10},{10,12},{12,14},{14,16},{16,18},{18... | collective-permute-start | bytes 245768 | tf_op jit(solution)/shard_map/ppermute | solution.py:17
  128.0 2.6 %collective-permute-done.16 = f32[10,4,1,512]{3,0,2,1:T(8,128)S(1)} collective-permute-done((f32[10,4,1,512]{3,0,2,1:T(8,128)S(1)}, f32[10,4,1,512]{3,0,2,1:T(8,128)S(1)}, u32[]{:S(2)}, u32[]{:S(2)}) %collective-permute-start.16) | collective-permute-done | bytes 81952 | tf_op jit(solution)/shard_map/ppermute | solution.py:20
  130.6 3.7 %collective-permute-done.17 = f32[10,4,1,512]{3,0,2,1:T(8,128)S(1)} collective-permute-done((f32[10,4,1,512]{3,0,2,1:T(8,128)S(1)}, f32[10,4,1,512]{3,0,2,1:T(8,128)S(1)}, u32[]{:S(2)}, u32[]{:S(2)}) %collective-permute-start.17) | collective-permute-done | bytes 81952 | tf_op jit(solution)/shard_map/ppermute | solution.py:17
  135.6 1.2 copy.20
  (69 shorter events, 15.0 us)
Async XLA Ops:
  8.3 24.6 %collective-permute-start = (f32[4,4,512]{2,1,0:T(4,128)S(1)}, f32[4,4,512]{2,1,0:T(4,128)S(1)}, u32[]{:S(2)}, u32[]{:S(2)}) collective-permute-start(f32[4,4,512]{2,1,0:T(4,128)S(1)} %get-tuple-element.20), channel_id=1, source_target_pairs={{0,2},{2,4},{4,6},{6,8},{8,10},{10,12},{12,14},{14,16},{16,18},{18... | collective-permute-start | bytes 98312 | tf_op jit(solution)/shard_map/ppermute | solution.py:17
  11.3 21.7 %collective-permute-start.1 = (f32[4,4,512]{2,1,0:T(4,128)S(1)}, f32[4,4,512]{2,1,0:T(4,128)S(1)}, u32[]{:S(2)}, u32[]{:S(2)}) collective-permute-start(f32[4,4,512]{2,1,0:T(4,128)S(1)} %get-tuple-element.21), channel_id=1, source_target_pairs={{2,0},{4,2},{6,4},{8,6},{10,8},{12,10},{14,12},{16,14},{18,16},{20... | collective-permute-start | bytes 98312 | tf_op jit(solution)/shard_map/ppermute | solution.py:20
  17.5 15.5 %collective-permute-start.2 = (f32[10,4,1,512]{3,0,2,1:T(8,128)}, f32[10,4,1,512]{3,0,2,1:T(8,128)S(1)}, u32[]{:S(2)}, u32[]{:S(2)}) collective-permute-start(f32[10,4,1,512]{3,0,2,1:T(8,128)} %get-tuple-element.19), channel_id=1, source_target_pairs={{2,0},{4,2},{6,4},{8,6},{10,8},{12,10},{14,12},{16,14},{18,16},{20... | collective-permute-start | bytes 245768 | tf_op jit(solution)/shard_map/ppermute | solution.py:20
  19.5 13.6 %collective-permute-start.3 = (f32[10,4,1,512]{3,0,2,1:T(8,128)S(1)}, f32[10,4,1,512]{3,0,2,1:T(8,128)S(1)}, u32[]{:S(2)}, u32[]{:S(2)}) collective-permute-start(f32[10,4,1,512]{3,0,2,1:T(8,128)S(1)} %get-tuple-element.18), channel_id=1, source_target_pairs={{0,2},{2,4},{4,6},{6,8},{8,10},{10,12},{12,14},{14,16},{16,18},{18... | collective-permute-start | bytes 245768 | tf_op jit(solution)/shard_map/ppermute | solution.py:17
  19.6 0.8 copy-start.2
  19.6 0.9 copy-start.3
  19.7 0.9 copy-start.4
  33.0 1.1 copy-start
  35.0 8.1 %collective-permute-start.4 = (f32[10,4,1,512]{3,0,2,1:T(8,128)S(1)}, f32[10,4,1,512]{3,0,2,1:T(8,128)S(1)}, u32[]{:S(2)}, u32[]{:S(2)}) collective-permute-start(f32[10,4,1,512]{3,0,2,1:T(8,128)S(1)} %get-tuple-element.17), channel_id=1, source_target_pairs={{2,0},{4,2},{6,4},{8,6},{10,8},{12,10},{14,12},{16,14},{18,16},{20... | collective-permute-start | bytes 245768 | tf_op jit(solution)/shard_map/ppermute | solution.py:20
  40.6 8.7 %collective-permute-start.5 = (f32[10,4,1,512]{3,0,2,1:T(8,128)S(1)}, f32[10,4,1,512]{3,0,2,1:T(8,128)S(1)}, u32[]{:S(2)}, u32[]{:S(2)}) collective-permute-start(f32[10,4,1,512]{3,0,2,1:T(8,128)S(1)} %get-tuple-element.16), channel_id=1, source_target_pairs={{0,2},{2,4},{4,6},{6,8},{8,10},{10,12},{12,14},{14,16},{16,18},{18... | collective-permute-start | bytes 245768 | tf_op jit(solution)/shard_map/ppermute | solution.py:17
  50.1 5.0 %collective-permute-start.6 = (f32[10,4,1,512]{3,0,2,1:T(8,128)S(1)}, f32[10,4,1,512]{3,0,2,1:T(8,128)S(1)}, u32[]{:S(2)}, u32[]{:S(2)}) collective-permute-start(f32[10,4,1,512]{3,0,2,1:T(8,128)S(1)} %get-tuple-element.15), channel_id=1, source_target_pairs={{2,0},{4,2},{6,4},{8,6},{10,8},{12,10},{14,12},{16,14},{18,16},{20... | collective-permute-start | bytes 245768 | tf_op jit(solution)/shard_map/ppermute | solution.py:20
  50.2 8.7 %collective-permute-start.7 = (f32[10,4,1,512]{3,0,2,1:T(8,128)S(1)}, f32[10,4,1,512]{3,0,2,1:T(8,128)S(1)}, u32[]{:S(2)}, u32[]{:S(2)}) collective-permute-start(f32[10,4,1,512]{3,0,2,1:T(8,128)S(1)} %get-tuple-element.14), channel_id=1, source_target_pairs={{0,2},{2,4},{4,6},{6,8},{8,10},{10,12},{12,14},{14,16},{16,18},{18... | collective-permute-start | bytes 245768 | tf_op jit(solution)/shard_map/ppermute | solution.py:17
  59.7 5.0 %collective-permute-start.8 = (f32[10,4,1,512]{3,0,2,1:T(8,128)S(1)}, f32[10,4,1,512]{3,0,2,1:T(8,128)S(1)}, u32[]{:S(2)}, u32[]{:S(2)}) collective-permute-start(f32[10,4,1,512]{3,0,2,1:T(8,128)S(1)} %get-tuple-element.13), channel_id=1, source_target_pairs={{2,0},{4,2},{6,4},{8,6},{10,8},{12,10},{14,12},{16,14},{18,16},{20... | collective-permute-start | bytes 245768 | tf_op jit(solution)/shard_map/ppermute | solution.py:20
  59.8 8.6 %collective-permute-start.9 = (f32[10,4,1,512]{3,0,2,1:T(8,128)S(1)}, f32[10,4,1,512]{3,0,2,1:T(8,128)S(1)}, u32[]{:S(2)}, u32[]{:S(2)}) collective-permute-start(f32[10,4,1,512]{3,0,2,1:T(8,128)S(1)} %get-tuple-element.12), channel_id=1, source_target_pairs={{0,2},{2,4},{4,6},{6,8},{8,10},{10,12},{12,14},{14,16},{16,18},{18... | collective-permute-start | bytes 245768 | tf_op jit(solution)/shard_map/ppermute | solution.py:17
  62.2 6.5 %copy-start.1 = (bf16[10,4,8,512]{3,2,1,0:T(8,128)(2,1)S(1)}, bf16[10,4,8,512]{3,2,1,0:T(8,128)(2,1)}, u32[]{:S(2)}) copy-start(bf16[10,4,8,512]{3,2,1,0:T(8,128)(2,1)} %param.10) | copy-start | bytes 983044
  69.5 14.3 %copy-start.5 = (f32[2048]{0:T(1024)S(1)}, f32[2048]{0:T(1024)}, u32[]{:S(2)}) copy-start(f32[2048]{0:T(1024)} %param.17) | copy-start | bytes 24580
  69.5 14.3 %copy-start.6 = (f32[2048]{0:T(1024)S(1)}, f32[2048]{0:T(1024)}, u32[]{:S(2)}) copy-start(f32[2048]{0:T(1024)} %param.16) | copy-start | bytes 24580
  95.9 6.4 %collective-permute-start.10 = (f32[10,4,1,512]{3,0,2,1:T(8,128)S(1)}, f32[10,4,1,512]{3,0,2,1:T(8,128)S(1)}, u32[]{:S(2)}, u32[]{:S(2)}) collective-permute-start(f32[10,4,1,512]{3,0,2,1:T(8,128)S(1)} %get-tuple-element.11), channel_id=1, source_target_pairs={{2,0},{4,2},{6,4},{8,6},{10,8},{12,10},{14,12},{16,14},{18,16},{20... | collective-permute-start | bytes 245768 | tf_op jit(solution)/shard_map/ppermute | solution.py:20
  96.0 9.2 %collective-permute-start.11 = (f32[10,4,1,512]{3,0,2,1:T(8,128)S(1)}, f32[10,4,1,512]{3,0,2,1:T(8,128)S(1)}, u32[]{:S(2)}, u32[]{:S(2)}) collective-permute-start(f32[10,4,1,512]{3,0,2,1:T(8,128)S(1)} %get-tuple-element.10), channel_id=1, source_target_pairs={{0,2},{2,4},{4,6},{6,8},{8,10},{10,12},{12,14},{14,16},{16,18},{18... | collective-permute-start | bytes 245768 | tf_op jit(solution)/shard_map/ppermute | solution.py:17
  106.1 6.2 %collective-permute-start.12 = (f32[10,4,1,512]{3,0,2,1:T(8,128)S(1)}, f32[10,4,1,512]{3,0,2,1:T(8,128)S(1)}, u32[]{:S(2)}, u32[]{:S(2)}) collective-permute-start(f32[10,4,1,512]{3,0,2,1:T(8,128)S(1)} %get-tuple-element.9), channel_id=1, source_target_pairs={{2,0},{4,2},{6,4},{8,6},{10,8},{12,10},{14,12},{16,14},{18,16},{20... | collective-permute-start | bytes 245768 | tf_op jit(solution)/shard_map/ppermute | solution.py:20
  106.5 8.6 %collective-permute-start.13 = (f32[10,4,1,512]{3,0,2,1:T(8,128)S(1)}, f32[10,4,1,512]{3,0,2,1:T(8,128)S(1)}, u32[]{:S(2)}, u32[]{:S(2)}) collective-permute-start(f32[10,4,1,512]{3,0,2,1:T(8,128)S(1)} %get-tuple-element.8), channel_id=1, source_target_pairs={{0,2},{2,4},{4,6},{6,8},{8,10},{10,12},{12,14},{14,16},{16,18},{18... | collective-permute-start | bytes 245768 | tf_op jit(solution)/shard_map/ppermute | solution.py:17
  115.8 5.2 %collective-permute-start.14 = (f32[10,4,1,512]{3,0,2,1:T(8,128)S(1)}, f32[10,4,1,512]{3,0,2,1:T(8,128)S(1)}, u32[]{:S(2)}, u32[]{:S(2)}) collective-permute-start(f32[10,4,1,512]{3,0,2,1:T(8,128)S(1)} %get-tuple-element.7), channel_id=1, source_target_pairs={{2,0},{4,2},{6,4},{8,6},{10,8},{12,10},{14,12},{16,14},{18,16},{20... | collective-permute-start | bytes 245768 | tf_op jit(solution)/shard_map/ppermute | solution.py:20
  116.2 8.7 %collective-permute-start.15 = (f32[10,4,1,512]{3,0,2,1:T(8,128)S(1)}, f32[10,4,1,512]{3,0,2,1:T(8,128)S(1)}, u32[]{:S(2)}, u32[]{:S(2)}) collective-permute-start(f32[10,4,1,512]{3,0,2,1:T(8,128)S(1)} %get-tuple-element.6), channel_id=1, source_target_pairs={{0,2},{2,4},{4,6},{6,8},{8,10},{10,12},{12,14},{14,16},{16,18},{18... | collective-permute-start | bytes 245768 | tf_op jit(solution)/shard_map/ppermute | solution.py:17
  125.6 5.0 %collective-permute-start.16 = (f32[10,4,1,512]{3,0,2,1:T(8,128)S(1)}, f32[10,4,1,512]{3,0,2,1:T(8,128)S(1)}, u32[]{:S(2)}, u32[]{:S(2)}) collective-permute-start(f32[10,4,1,512]{3,0,2,1:T(8,128)S(1)} %get-tuple-element.5), channel_id=1, source_target_pairs={{2,0},{4,2},{6,4},{8,6},{10,8},{12,10},{14,12},{16,14},{18,16},{20... | collective-permute-start | bytes 245768 | tf_op jit(solution)/shard_map/ppermute | solution.py:20
  125.7 8.6 %collective-permute-start.17 = (f32[10,4,1,512]{3,0,2,1:T(8,128)S(1)}, f32[10,4,1,512]{3,0,2,1:T(8,128)S(1)}, u32[]{:S(2)}, u32[]{:S(2)}) collective-permute-start(f32[10,4,1,512]{3,0,2,1:T(8,128)S(1)} %get-tuple-element.4), channel_id=1, source_target_pairs={{0,2},{2,4},{4,6},{6,8},{8,10},{10,12},{12,14},{14,16},{16,18},{18... | collective-permute-start | bytes 245768 | tf_op jit(solution)/shard_map/ppermute | solution.py:17
where the time goes:
time: 137 us
  waiting for transfers between devices  46.6 us (34%)
  local copies, waits for them, and re-layouts  30.2 us (22%)
  other arithmetic  29.1 us (21%)
  starting transfers between devices  27.3 us (20%)
  blocking collectives  2.5 us (2%)
    ppermute x9, waiting for transfers between devices, padded_2(): lax.ppermute(lax.slice_in_dim(block, block.shape[dim] - width, None, axis...  26.7 us
    ppermute x9, waiting for transfers between devices, padded_2(): lax.ppermute(lax.slice_in_dim(block, 0, width, axis=dim), axis, backward)  19.9 us
    ppermute x9, starting transfers between devices, padded_2(): lax.ppermute(lax.slice_in_dim(block, block.shape[dim] - width, None, axis...  14.7 us
    ppermute x9, starting transfers between devices, padded_2(): lax.ppermute(lax.slice_in_dim(block, 0, width, axis=dim), axis, backward)  12.6 us
    gather x1, local copies, waits for them, and re-layouts, per_device(): local_vals = partial_value.reshape(-1)[obs_cell]  11.8 us
    gather x1, local copies, waits for them, and re-layouts, per_device(): values = (sigma * static_ctl).reshape(-1)[obs_cell] + scale * summed  11.8 us
    scatter-add x1, other arithmetic, per_device(): adjoint = jnp.zeros((partial_value.size,), jnp.float32).at[obs_cell].add(...  11.4 us
    select_n x1, other arithmetic, lookup(): coeff = jnp.where(class_index == number, class_kappa[number], coeff)  6.03 us
  transfers between devices with their start and end apart: 18, of which 14 were waited for; matrix products, arithmetic and copies ran while one was open for 13% of the time, Pallas kernels for 0%

commit v1 on v0

v1 whole, which is shorter than its diff:
```python
import functools
import math

import jax
import jax.numpy as jnp
from jax import lax
from jax.experimental import pallas as pl
from jax.experimental.pallas import tpu as pltpu
from jax.sharding import PartitionSpec as P

PASSES = 4
MESH = pl.DeviceIdType.MESH
LANES = 128
PIECES = 3
CHUNKS = 2


def sublane(shape):
    return lax.broadcasted_iota(jnp.int32, shape, len(shape) - 2)


def roll(x, shift, axis):
    return pltpu.roll(x, shift, axis % x.ndim)


def toward_right(own, halo):
    last = sublane(own.shape) == 7
    a, b = roll(own, 7, -2), roll(halo, 7, -2)
    return jnp.where(last, b, a), jnp.where(last, a, b)


def toward_left(own, halo):
    first = sublane(own.shape) == 0
    a, b = roll(own, 1, -2), roll(halo, 1, -2)
    return jnp.where(first, b, a), jnp.where(first, a, b)


def pack(a, b):
    top = sublane(a.shape) < 4
    return jnp.where(top, a, roll(b, 4, -2)), jnp.where(top, roll(a, 4, -2), b)


def faces(own, halo):
    right_own, right_halo = toward_right(own, halo)
    rows = own.shape[-1]
    inside = lax.broadcasted_iota(jnp.int32, own.shape, own.ndim - 1) < rows - 1
    zero = jnp.zeros_like(own)
    fx_own = 0.5 * (own + right_own)
    fx_halo = jnp.where(sublane(own.shape) == 3, zero, 0.5 * (halo + right_halo))
    fy_own = jnp.where(inside, 0.5 * (own + roll(own, rows - 1, -1)), zero)
    fy_halo = jnp.where(inside, 0.5 * (halo + roll(halo, rows - 1, -1)), zero)
    return fx_own, fx_halo, fy_own, fy_halo


def diffuse(own, halo, fx_own, fx_halo, fy_own, fy_halo):
    rows = own.shape[-1]
    for _ in range(PASSES):
        right_own, right_halo = toward_right(own, halo)
        flux_own = fx_own * (right_own - own)
        flux_halo = fx_halo * (right_halo - halo)
        left_own, left_halo = toward_left(flux_own, flux_halo)
        up_own = fy_own * (roll(own, rows - 1, -1) - own)
        up_halo = fy_halo * (roll(halo, rows - 1, -1) - halo)
        own = own + (flux_own - left_own) + (up_own - roll(up_own, 1, -1))
        halo = halo + (flux_halo - left_halo) + (up_halo - roll(up_halo, 1, -1))
    return own, halo


def split3(x):
    out = []
    for _ in range(PIECES):
        piece = x.astype(jnp.bfloat16)
        out.append(piece.astype(jnp.float32))
        x = x - out[-1]
    return out


def scatter(cell, weight, product, hot_hi, hot_lo):
    groups = cell.shape[0]
    spot = lax.broadcasted_iota(jnp.int32, (LANES, LANES), 0)
    for g in range(groups):
        c = cell[g : g + 1, :]
        hi = (c // 4096) * 32 + ((c // 128) % 4) * 8 + (c // 512) % 8
        lo = c % 128
        lanes = slice(g * LANES, (g + 1) * LANES)
        hot_hi[:, lanes] = (spot == hi).astype(jnp.float32).astype(jnp.bfloat16)
        here = spot == lo
        values = split3(weight[g : g + 1, :]) + split3(product[g : g + 1, :])
        for i, value in enumerate(values):
            hot_lo[i * LANES : (i + 1) * LANES, lanes] = jnp.where(here, value, 0.0).astype(
                jnp.bfloat16
            )


def exchange(
    n_dom, n_ens, scale,
    kappa, alpha, perturb, static, sigma, index, obs_cell, obs_value, obs_weight,
    adj_out, ph_out, fx_out, fy_out,
    c_send, c_recv, p_send, p_recv, e_send, e_recv, a_send, a_recv, total,
    tail, weights, hot_hi, hot_lo,
    c_ss, c_rs, p_ss, p_rs, e_ss, e_rs, a_ss, a_rs, t_ss, t_rs,
):
    me, ens = lax.axis_index("dom"), lax.axis_index("ens")
    right, left = lax.rem(me + 1, n_dom), lax.rem(me + n_dom - 1, n_dom)
    members, levels = alpha.shape[0], alpha.shape[1]
    rows = alpha.shape[3]

    barrier = pltpu.get_barrier_semaphore()
    for side in (left, right):
        pl.semaphore_signal(barrier, inc=1, device_id=(side, ens), device_id_type=MESH)
    for r in range(1, n_ens):
        pl.semaphore_signal(
            barrier, inc=1, device_id=(me, lax.rem(ens + r, n_ens)), device_id_type=MESH
        )

    def send(src, dst, ss, rs, side):
        copy = pltpu.make_async_remote_copy(
            src_ref=src, dst_ref=dst, send_sem=ss, recv_sem=rs,
            device_id=(side, ens), device_id_type=MESH,
        )
        copy.start()
        return copy

    cls = index[...]
    coeff = jnp.zeros(cls.shape, jnp.float32)
    for number in range(kappa.shape[0]):
        coeff = jnp.where(cls == number, kappa[number], coeff)
    for pair in range(levels // 2):
        low, high = pack(coeff[2 * pair], coeff[2 * pair + 1])
        c_send[0, pair] = low
        c_send[1, pair] = high
    pl.semaphore_wait(barrier, 2 + n_ens - 1)
    coeff_copies = [
        send(c_send.at[s], c_recv.at[s], c_ss.at[s], c_rs.at[s], side)
        for s, side in ((0, left), (1, right))
    ]
    part = members // CHUNKS
    halo_copies = []
    for chunk in range(CHUNKS):
        def fill(m, carry):
            for pair in range(levels // 2):
                a = perturb[m, 2 * pair].astype(jnp.float32)
                b = perturb[m, 2 * pair + 1].astype(jnp.float32)
                low, high = pack(a, b)
                p_send[0, m, pair] = low
                p_send[1, m, pair] = high
            return carry

        lax.fori_loop(chunk * part, (chunk + 1) * part, fill, 0)
        span = pl.ds(chunk * part, part)
        halo_copies.append([
            send(p_send.at[s, span], p_recv.at[s, span],
                 p_ss.at[s, chunk], p_rs.at[s, chunk], side)
            for s, side in ((0, left), (1, right))
        ])

    scatter(
        obs_cell[...], obs_weight[...], obs_weight[...] * obs_value[...], hot_hi, hot_lo
    )
    sums = lax.dot_general(
        hot_hi[...], hot_lo[...], (((1,), (1,)), ((), ())), preferred_element_type=jnp.float32
    )
    for which in range(2):
        whole = sums[:, which * PIECES * LANES : (which * PIECES + 1) * LANES]
        for i in range(1, PIECES):
            at = (which * PIECES + i) * LANES
            whole = whole + sums[:, at : at + LANES]
        for level in range(levels):
            for block in range(rows // LANES):
                at = (level * (rows // LANES) + block) * 8
                weights[which, level, :, block * LANES : (block + 1) * LANES] = whole[at : at + 8]

    for copy in coeff_copies:
        copy.wait()
    for pair in range(levels // 2):
        for i in range(2):
            level = 2 * pair + i
            halo = halo_tile(c_recv[0, pair], c_recv[1, pair], i)
            f = faces(coeff[level], halo)
            fx_out[0, level], fx_out[1, level], fy_out[0, level], fy_out[1, level] = f

    for level in range(levels):
        f = (fx_out[0, level], fx_out[1, level], fy_out[0, level], fy_out[1, level])

        def smooth(m, acc):
            own, halo = diffuse(
                alpha[m, level], jnp.zeros((8, rows), jnp.float32), *f
            )
            tail[m, level] = halo
            return acc + perturb[m, level].astype(jnp.float32) * own

        total[0, level] = lax.fori_loop(
            0, members, smooth, jnp.zeros((8, rows), jnp.float32), unroll=2
        )

    edge = [jnp.zeros((8, rows), jnp.float32)] * levels
    for chunk in range(CHUNKS):
        for copy in halo_copies[chunk]:
            copy.wait()

        def gather(m, acc):
            out = []
            for level in range(levels):
                halo = halo_tile(p_recv[0, m, level // 2], p_recv[1, m, level // 2], level % 2)
                ph_out[m, level] = halo
                out.append(acc[level] + halo * tail[m, level])
            return tuple(out)

        edge = lax.fori_loop(chunk * part, (chunk + 1) * part, gather, tuple(edge))
    for pair in range(levels // 2):
        low, high = pack(edge[2 * pair], edge[2 * pair + 1])
        e_send[0, pair] = low
        e_send[1, pair] = high
    edge_copies = [
        send(e_send.at[s], e_recv.at[s], e_ss.at[s], e_rs.at[s], side)
        for s, side in ((0, right), (1, left))
    ]
    for copy in edge_copies:
        copy.wait()
    for level in range(levels):
        total[0, level] = total[0, level] + halo_tile(
            e_recv[0, level // 2], e_recv[1, level // 2], level % 2
        )
    sums_copies = []
    for r in range(1, n_ens):
        copy = pltpu.make_async_remote_copy(
            src_ref=total.at[0], dst_ref=total.at[r],
            send_sem=t_ss.at[r], recv_sem=t_rs.at[r],
            device_id=(me, lax.rem(ens + r, n_ens)), device_id_type=MESH,
        )
        copy.start()
        sums_copies.append(copy)
    for copy in sums_copies:
        copy.wait()
    increment = total[lax.rem(ens + n_ens, n_ens)]
    for j in range(1, n_ens):
        increment = increment + total[lax.rem(ens - j + n_ens, n_ens)]
    state = sigma[...] * static[...] + scale * increment
    adjoint = weights[0] * state - weights[1]
    adj_out[0] = adjoint
    for pair in range(levels // 2):
        low, high = pack(adjoint[2 * pair], adjoint[2 * pair + 1])
        a_send[0, pair] = low
        a_send[1, pair] = high
    adjoint_copies = [
        send(a_send.at[s], a_recv.at[s], a_ss.at[s], a_rs.at[s], side)
        for s, side in ((0, left), (1, right))
    ]
    for copy in adjoint_copies:
        copy.wait()
    for level in range(levels):
        adj_out[1, level] = halo_tile(a_recv[0, level // 2], a_recv[1, level // 2], level % 2)


def halo_tile(first, second, i):
    top = sublane(first.shape) < 4
    if i == 0:
        return jnp.where(top, first, roll(second, 4, -2))
    return jnp.where(top, roll(first, 4, -2), second)


def finish(scale, alpha, perturb, ph, adj, fx, fy, static, sigma, ga, gs):
    @pl.when(pl.program_id(0) == 0)
    def _():
        gs[...] = static[...] + sigma[...] * adj[0]

    for m in range(alpha.shape[0]):
        for level in range(alpha.shape[1]):
            own = perturb[m, level].astype(jnp.float32) * adj[0, level]
            halo = ph[m, level] * adj[1, level]
            own, halo = diffuse(
                own, halo, fx[0, level], fx[1, level], fy[0, level], fy[1, level]
            )
            ga[m, level] = alpha[m, level] + scale * own


def per_device(
    alpha, perturb, static_ctl, sigma, class_index, class_kappa, obs_cell, obs_value, obs_weight
):
    n_dom, n_ens = lax.axis_size("dom"), lax.axis_size("ens")
    local, levels, columns, rows = alpha.shape
    assert columns == 8 and levels == 4 and rows == 512
    scale = 1.0 / math.sqrt(local * n_ens - 1)
    groups = obs_cell.shape[0] // LANES
    f32 = jnp.float32
    tile = (levels, columns, rows)
    half = (2, levels // 2, columns, rows)
    vmem = pl.BlockSpec(memory_space=pltpu.VMEM)
    dma = pltpu.SemaphoreType.DMA
    adj, ph, fx, fy = pl.pallas_call(
        functools.partial(exchange, n_dom, n_ens, scale),
        out_shape=(
            jax.ShapeDtypeStruct((2,) + tile, f32),
            jax.ShapeDtypeStruct((local,) + tile, f32),
            jax.ShapeDtypeStruct((2,) + tile, f32),
            jax.ShapeDtypeStruct((2,) + tile, f32),
        ),
        in_specs=[pl.BlockSpec(memory_space=pltpu.SMEM)] + [vmem] * 8,
        out_specs=(vmem,) * 4,
        scratch_shapes=[
            pltpu.VMEM(half, f32),
            pltpu.VMEM(half, f32),
            pltpu.VMEM((2, local) + half[1:], f32),
            pltpu.VMEM((2, local) + half[1:], f32),
            pltpu.VMEM(half, f32),
            pltpu.VMEM(half, f32),
            pltpu.VMEM(half, f32),
            pltpu.VMEM(half, f32),
            pltpu.VMEM((n_ens,) + tile, f32),
            pltpu.VMEM((local,) + tile, f32),
            pltpu.VMEM((2,) + tile, f32),
            pltpu.VMEM((LANES, groups * LANES), jnp.bfloat16),
            pltpu.VMEM((2 * PIECES * LANES, groups * LANES), jnp.bfloat16),
            dma((2,)), dma((2,)),
            dma((2, CHUNKS)), dma((2, CHUNKS)),
            dma((2,)), dma((2,)),
            dma((2,)), dma((2,)),
            dma((n_ens,)), dma((n_ens,)),
        ],
        compiler_params=pltpu.CompilerParams(
            collective_id=0, has_side_effects=True, vmem_limit_bytes=40 * 2**20
        ),
        name="exchange",
    )(
        class_kappa, alpha, perturb, static_ctl, sigma, class_index,
        obs_cell.reshape(groups, LANES), obs_value.reshape(groups, LANES),
        obs_weight.reshape(groups, LANES),
    )
    block = 2
    moving = pl.BlockSpec((block,) + tile, lambda i: (i, 0, 0, 0))
    fixed = pl.BlockSpec((2,) + tile, lambda i: (0, 0, 0, 0))
    plain = pl.BlockSpec(tile, lambda i: (0, 0, 0))
    return pl.pallas_call(
        functools.partial(finish, scale),
        out_shape=(
            jax.ShapeDtypeStruct(alpha.shape, f32),
            jax.ShapeDtypeStruct(static_ctl.shape, f32),
        ),
        grid=(local // block,),
        in_specs=[moving, moving, moving, fixed, fixed, fixed, plain, plain],
        out_specs=(moving, plain),
        name="finish",
    )(alpha, perturb, ph, adj, fx, fy, static_ctl, sigma)


def solution(mesh):
    return jax.shard_map(
        per_device,
        mesh=mesh,
        in_specs=(
            P("ens", None, "dom", None),
            P("ens", None, "dom", None),
            P(None, "dom", None),
            P(None, "dom", None),
            P(None, "dom", None),
            P(),
            P("dom"),
            P("dom"),
            P("dom"),
        ),
        out_specs=(P("ens", None, "dom", None), P(None, "dom", None)),
        check_vma=False,
    )
```

time: 137 us -> 56 us (0.41)
  waiting for transfers between devices: 46.6 us -> 0 us
  Pallas kernels: 0 us -> 44.6 us
  other arithmetic: 29.1 us -> 0 us
  starting transfers between devices: 27.3 us -> 0 us
  local copies, waits for them, and re-layouts: 30.2 us -> 10.1 us
  blocking collectives: 2.5 us -> 0 us
    ppermute x18 -> x0, waiting for transfers between devices: 46.6 us -> none  [the longest x9 26.7 us: padded_2(): lax.ppermute(lax.slice_in_dim(block, block.shape[dim] - width, None, axis...]
    pallas_call x0 -> x2, Pallas kernels: none -> 44.6 us  [the longest x1 38 us: per_device(): pl.pallas_call(functools.partial(exchange, n_dom, n_ens, scale), out_shap...]
    ppermute x18 -> x0, starting transfers between devices: 27.3 us -> none  [the longest x9 14.7 us: padded_2(): lax.ppermute(lax.slice_in_dim(block, block.shape[dim] - width, None, axis...]
    gather x2 -> x0, local copies, waits for them, and re-layouts: 23.6 us -> none  [the longest x1 11.8 us: per_device(): local_vals = partial_value.reshape(-1)[obs_cell]]
    scatter-add x1 -> x0, other arithmetic: 11.4 us -> none  [per_device(): adjoint = jnp.zeros((partial_value.size,), jnp.float32).at[obs_cell].add(...]
    select_n x1 -> x0, other arithmetic: 6.03 us -> none  [lookup(): coeff = jnp.where(class_index == number, class_kappa[number], coeff)]
    unnamed x18 -> x26, local copies, waits for them, and re-layouts: 4.13 us -> 10.1 us
    add x8 -> x0, other arithmetic: 5.37 us -> none  [the longest x6 3.66 us: one_pass(): inner + (flux_x[..., 1:, :] - flux_x[..., :-1, :])]
  transfers between devices with their start and end apart: 18 -> 0, of which waited for: 14 -> 0; matrix products, arithmetic and copies ran while one was open for 13% -> 0% of each run, Pallas kernels for 0% -> 0%
where the time goes in v1:
time: 56 us; the launch traced here: 55.4 us
  Pallas kernels  44.6 us (80%)
  local copies, waits for them, and re-layouts  10.1 us (18%)
  between operations  0.67 us (1%)
    pallas_call x1, Pallas kernels, per_device(): pl.pallas_call(functools.partial(exchange, n_dom, n_ens, scale), out_shap...  38 us
    unnamed x26, local copies, waits for them, and re-layouts  10.1 us
    pallas_call x1, Pallas kernels, per_device(): pl.pallas_call(functools.partial(finish, scale), out_shape=(jax.ShapeDtyp...  6.63 us

profile of v1, /device:TPU:0, one launch (start us, length us, event | category | flops | bytes accessed | tf_op | source)
XLA Modules:
  0.0 55.4 jit_solution(9032628899946878524)
XLA Ops:
  0.6 0.0 copy-start.12
  0.6 0.6 %copy-done.12 = f32[8]{0:T(128)S(1)} copy-done((f32[8]{0:T(128)S(1)}, f32[8]{0:T(128)}, u32[]{:S(2)}) %copy-start.12) | copy-done | bytes 56
  1.3 0.0 copy-start
  1.3 1.1 %copy-done = f32[10,4,8,512]{3,2,1,0:T(8,128)S(1)} copy-done((f32[10,4,8,512]{3,2,1,0:T(8,128)S(1)}, f32[10,4,8,512]{3,2,1,0:T(8,128)}, u32[]{:S(2)}) %copy-start) | copy-done | bytes 655384
  2.4 0.0 copy-start.1
  2.4 1.0 %copy-done.1 = bf16[10,4,8,512]{3,2,1,0:T(8,128)(2,1)S(1)} copy-done((bf16[10,4,8,512]{3,2,1,0:T(8,128)(2,1)S(1)}, bf16[10,4,8,512]{3,2,1,0:T(8,128)(2,1)}, u32[]{:S(2)}) %copy-start.1) | copy-done | bytes 327704
  3.3 0.0 copy-start.3
  3.4 0.8 %copy-done.3 = f32[4,8,512]{2,1,0:T(8,128)S(1)} copy-done((f32[4,8,512]{2,1,0:T(8,128)S(1)}, f32[4,8,512]{2,1,0:T(8,128)}, u32[]{:S(2)}) %copy-start.3) | copy-done | bytes 65560
  4.2 0.0 copy-start.4
  4.2 0.8 %copy-done.4 = f32[4,8,512]{2,1,0:T(8,128)S(1)} copy-done((f32[4,8,512]{2,1,0:T(8,128)S(1)}, f32[4,8,512]{2,1,0:T(8,128)}, u32[]{:S(2)}) %copy-start.4) | copy-done | bytes 65560
  5.0 0.0 copy-start.8
  5.0 0.8 %copy-done.8 = s32[4,8,512]{2,1,0:T(8,128)S(1)} copy-done((s32[4,8,512]{2,1,0:T(8,128)S(1)}, s32[4,8,512]{2,1,0:T(8,128)}, u32[]{:S(2)}) %copy-start.8) | copy-done | bytes 65560
  5.9 0.0 copy-start.9
  5.9 0.7 %copy-done.9 = s32[2048]{0:T(1024)S(1)} copy-done((s32[2048]{0:T(1024)S(1)}, s32[2048]{0:T(1024)}, u32[]{:S(2)}) %copy-start.9) | copy-done | bytes 8216
  6.6 0.0 copy-start.10
  6.6 0.7 %copy-done.10 = f32[2048]{0:T(1024)S(1)} copy-done((f32[2048]{0:T(1024)S(1)}, f32[2048]{0:T(1024)}, u32[]{:S(2)}) %copy-start.10) | copy-done | bytes 8216
  7.3 0.0 copy-start.11
  7.3 0.7 %copy-done.11 = f32[2048]{0:T(1024)S(1)} copy-done((f32[2048]{0:T(1024)S(1)}, f32[2048]{0:T(1024)}, u32[]{:S(2)}) %copy-start.11) | copy-done | bytes 8216
  8.0 38.0 %exchange.1 = (f32[2,4,8,512]{3,2,1,0:T(8,128)S(1)}, f32[10,4,8,512]{3,2,1,0:T(8,128)S(1)}, f32[2,4,8,512]{3,2,1,0:T(8,128)S(1)}, f32[2,4,8,512]{3,2,1,0:T(8,128)S(1)}) custom-call(f32[8]{0:T(128)S(1)} %copy-done.12, f32[10,4,8,512]{3,2,1,0:T(8,128)S(1)} %copy-done, bf16[10,4,8,512]{3,2,1,0:T(8,128)(2,1)S(1)} %copy-done.1, f32[4,8,512]{2,1,0:T(8,128)S(1)} %copy-done.3, ...), custom_call_target="tpu_custom_call" | custom-call | tf_op jit(solution)/shard_map/exchange/pallas_call | solution.py:290
  46.0 0.0 copy-start.2
  46.0 0.8 %copy-done.2 = f32[10,4,8,512]{3,2,1,0:T(8,128)} copy-done((f32[10,4,8,512]{3,2,1,0:T(8,128)}, f32[10,4,8,512]{3,2,1,0:T(8,128)S(1)}, u32[]{:S(2)}) %copy-start.2) | copy-done | bytes 655384
  46.8 0.0 copy-start.5
  46.8 0.7 %copy-done.5 = f32[2,4,8,512]{3,2,1,0:T(8,128)} copy-done((f32[2,4,8,512]{3,2,1,0:T(8,128)}, f32[2,4,8,512]{3,2,1,0:T(8,128)S(1)}, u32[]{:S(2)}) %copy-start.5) | copy-done | bytes 131096
  47.5 0.0 copy-start.6
  47.5 0.7 %copy-done.6 = f32[2,4,8,512]{3,2,1,0:T(8,128)} copy-done((f32[2,4,8,512]{3,2,1,0:T(8,128)}, f32[2,4,8,512]{3,2,1,0:T(8,128)S(1)}, u32[]{:S(2)}) %copy-start.6) | copy-done | bytes 131096
  48.1 0.0 copy-start.7
  48.2 0.6 %copy-done.7 = f32[2,4,8,512]{3,2,1,0:T(8,128)} copy-done((f32[2,4,8,512]{3,2,1,0:T(8,128)}, f32[2,4,8,512]{3,2,1,0:T(8,128)S(1)}, u32[]{:S(2)}) %copy-start.7) | copy-done | bytes 131096
  48.8 6.6 %finish.1 = (f32[10,4,8,512]{3,2,1,0:T(8,128)}, f32[4,8,512]{2,1,0:T(8,128)}) custom-call(f32[10,4,8,512]{3,2,1,0:T(8,128)} %alpha.3, bf16[10,4,8,512]{3,2,1,0:T(8,128)(2,1)} %perturb.3, f32[10,4,8,512]{3,2,1,0:T(8,128)} %copy-done.2, f32[2,4,8,512]{3,2,1,0:T(8,128)} %copy-done.5, f32[2,4,8,512]{3,2,1,0:T(8,128)} %copy-done.6, f32[2,4,8,512]{3,2,1,0:T(8,128)} %copy-done.7, ...), custom_call_target="tpu_custom_call" | custom-call | tf_op jit(solution)/shard_map/finish/pallas_call | solution.py:333
Async XLA Ops:
  0.6 0.7 %copy-start.12 = (f32[8]{0:T(128)S(1)}, f32[8]{0:T(128)}, u32[]{:S(2)}) copy-start(f32[8]{0:T(128)} %kappa.1) | copy-start | bytes 100
  1.3 1.1 %copy-start = (f32[10,4,8,512]{3,2,1,0:T(8,128)S(1)}, f32[10,4,8,512]{3,2,1,0:T(8,128)}, u32[]{:S(2)}) copy-start(f32[10,4,8,512]{3,2,1,0:T(8,128)} %alpha.3) | copy-start | bytes 1966084
  2.4 1.0 %copy-start.1 = (bf16[10,4,8,512]{3,2,1,0:T(8,128)(2,1)S(1)}, bf16[10,4,8,512]{3,2,1,0:T(8,128)(2,1)}, u32[]{:S(2)}) copy-start(bf16[10,4,8,512]{3,2,1,0:T(8,128)(2,1)} %perturb.3) | copy-start | bytes 983044
  3.3 0.8 %copy-start.3 = (f32[4,8,512]{2,1,0:T(8,128)S(1)}, f32[4,8,512]{2,1,0:T(8,128)}, u32[]{:S(2)}) copy-start(f32[4,8,512]{2,1,0:T(8,128)} %static.3) | copy-start | bytes 196612
  4.2 0.8 %copy-start.4 = (f32[4,8,512]{2,1,0:T(8,128)S(1)}, f32[4,8,512]{2,1,0:T(8,128)}, u32[]{:S(2)}) copy-start(f32[4,8,512]{2,1,0:T(8,128)} %sigma.3) | copy-start | bytes 196612
  5.0 0.8 %copy-start.8 = (s32[4,8,512]{2,1,0:T(8,128)S(1)}, s32[4,8,512]{2,1,0:T(8,128)}, u32[]{:S(2)}) copy-start(s32[4,8,512]{2,1,0:T(8,128)} %index.1) | copy-start | bytes 196612
  5.9 0.7 %copy-start.9 = (s32[2048]{0:T(1024)S(1)}, s32[2048]{0:T(1024)}, u32[]{:S(2)}) copy-start(s32[2048]{0:T(1024)} %param.15) | copy-start | bytes 24580
  6.6 0.7 %copy-start.10 = (f32[2048]{0:T(1024)S(1)}, f32[2048]{0:T(1024)}, u32[]{:S(2)}) copy-start(f32[2048]{0:T(1024)} %param.16) | copy-start | bytes 24580
  7.3 0.7 %copy-start.11 = (f32[2048]{0:T(1024)S(1)}, f32[2048]{0:T(1024)}, u32[]{:S(2)}) copy-start(f32[2048]{0:T(1024)} %param.17) | copy-start | bytes 24580
  46.0 0.9 %copy-start.2 = (f32[10,4,8,512]{3,2,1,0:T(8,128)}, f32[10,4,8,512]{3,2,1,0:T(8,128)S(1)}, u32[]{:S(2)}) copy-start(f32[10,4,8,512]{3,2,1,0:T(8,128)S(1)} %get-tuple-element.6.ph) | copy-start | bytes 1966084
  46.8 0.7 %copy-start.5 = (f32[2,4,8,512]{3,2,1,0:T(8,128)}, f32[2,4,8,512]{3,2,1,0:T(8,128)S(1)}, u32[]{:S(2)}) copy-start(f32[2,4,8,512]{3,2,1,0:T(8,128)S(1)} %get-tuple-element.7.adj) | copy-start | bytes 393220
  47.5 0.7 %copy-start.6 = (f32[2,4,8,512]{3,2,1,0:T(8,128)}, f32[2,4,8,512]{3,2,1,0:T(8,128)S(1)}, u32[]{:S(2)}) copy-start(f32[2,4,8,512]{3,2,1,0:T(8,128)S(1)} %get-tuple-element.8.fx) | copy-start | bytes 393220
  48.1 0.6 %copy-start.7 = (f32[2,4,8,512]{3,2,1,0:T(8,128)}, f32[2,4,8,512]{3,2,1,0:T(8,128)S(1)}, u32[]{:S(2)}) copy-start(f32[2,4,8,512]{3,2,1,0:T(8,128)S(1)} %get-tuple-element.9.fy) | copy-start | bytes 393220

commit v2 on v1

--- a/solution.py
+++ b/solution.py
@@ -12,7 +12,8 @@
 MESH = pl.DeviceIdType.MESH
 LANES = 128
 PIECES = 3
-CHUNKS = 2
+CHUNKS = 5
+BATCH = 2
 
 
 def sublane(shape):
@@ -94,16 +95,33 @@
 
 def exchange(
     n_dom, n_ens, scale,
-    kappa, alpha, perturb, static, sigma, index, obs_cell, obs_value, obs_weight,
-    adj_out, ph_out, fx_out, fy_out,
+    kappa_in, alpha_in, perturb_in, static_in, sigma_in, index_in, cell_in, value_in, weight_in,
+    ga, gs,
+    adj_out, ph_out, fx_out, fy_out, alpha, perturb, gs_out, kappa, static, sigma, index, obs_cell, obs_value, obs_weight,
     c_send, c_recv, p_send, p_recv, e_send, e_recv, a_send, a_recv, total,
     tail, weights, hot_hi, hot_lo,
-    c_ss, c_rs, p_ss, p_rs, e_ss, e_rs, a_ss, a_rs, t_ss, t_rs,
+    in_sem, pin_sem, ga_sem, gs_sem, c_ss, c_rs, p_ss, p_rs, e_ss, e_rs, a_ss, a_rs, t_ss, t_rs,
 ):
     me, ens = lax.axis_index("dom"), lax.axis_index("ens")
     right, left = lax.rem(me + 1, n_dom), lax.rem(me + n_dom - 1, n_dom)
     members, levels = alpha.shape[0], alpha.shape[1]
     rows = alpha.shape[3]
+
+    part = members // CHUNKS
+    loads = []
+    for i, (src, dst) in enumerate((
+        (kappa_in, kappa), (index_in, index), (cell_in, obs_cell), (value_in, obs_value),
+        (weight_in, obs_weight), (static_in, static), (sigma_in, sigma), (alpha_in, alpha),
+    )):
+        loads.append(pltpu.make_async_copy(src, dst, in_sem.at[i]))
+    perturb_loads = [
+        pltpu.make_async_copy(
+            perturb_in.at[pl.ds(c * part, part)], perturb.at[pl.ds(c * part, part)], pin_sem.at[c]
+        )
+        for c in range(CHUNKS)
+    ]
+    for copy in loads[:2] + perturb_loads + loads[2:]:
+        copy.start()
 
     barrier = pltpu.get_barrier_semaphore()
     for side in (left, right):
@@ -121,6 +139,8 @@
         copy.start()
         return copy
 
+    loads[0].wait()
+    loads[1].wait()
     cls = index[...]
     coeff = jnp.zeros(cls.shape, jnp.float32)
     for number in range(kappa.shape[0]):
@@ -134,9 +154,10 @@
         send(c_send.at[s], c_recv.at[s], c_ss.at[s], c_rs.at[s], side)
         for s, side in ((0, left), (1, right))
     ]
-    part = members // CHUNKS
     halo_copies = []
     for chunk in range(CHUNKS):
+        perturb_loads[chunk].wait()
+
         def fill(m, carry):
             for pair in range(levels // 2):
                 a = perturb[m, 2 * pair].astype(jnp.float32)
@@ -154,6 +175,8 @@
             for s, side in ((0, left), (1, right))
         ])
 
+    for copy in loads[2:5]:
+        copy.wait()
     scatter(
         obs_cell[...], obs_weight[...], obs_weight[...] * obs_value[...], hot_hi, hot_lo
     )
@@ -179,18 +202,18 @@
             f = faces(coeff[level], halo)
             fx_out[0, level], fx_out[1, level], fy_out[0, level], fy_out[1, level] = f
 
+    loads[7].wait()
     for level in range(levels):
         f = (fx_out[0, level], fx_out[1, level], fy_out[0, level], fy_out[1, level])
 
-        def smooth(m, acc):
-            own, halo = diffuse(
-                alpha[m, level], jnp.zeros((8, rows), jnp.float32), *f
-            )
-            tail[m, level] = halo
-            return acc + perturb[m, level].astype(jnp.float32) * own
+        def smooth(i, acc):
+            span = pl.ds(i * BATCH, BATCH)
+            own, halo = diffuse(alpha[span, level], jnp.zeros((BATCH, 8, rows), jnp.float32), *f)
+            tail[span, level] = halo
+            return acc + jnp.sum(perturb[span, level].astype(jnp.float32) * own, axis=0)
 
         total[0, level] = lax.fori_loop(
-            0, members, smooth, jnp.zeros((8, rows), jnp.float32), unroll=2
+            0, members // BATCH, smooth, jnp.zeros((8, rows), jnp.float32)
         )
 
     edge = [jnp.zeros((8, rows), jnp.float32)] * levels
@@ -235,6 +258,8 @@
     increment = total[lax.rem(ens + n_ens, n_ens)]
     for j in range(1, n_ens):
         increment = increment + total[lax.rem(ens - j + n_ens, n_ens)]
+    loads[5].wait()
+    loads[6].wait()
     state = sigma[...] * static[...] + scale * increment
     adjoint = weights[0] * state - weights[1]
     adj_out[0] = adjoint
@@ -246,10 +271,31 @@
         send(a_send.at[s], a_recv.at[s], a_ss.at[s], a_rs.at[s], side)
         for s, side in ((0, left), (1, right))
     ]
+    gs_out[...] = static[...] + sigma[...] * adjoint
+    gs_copy = pltpu.make_async_copy(gs_out, gs, gs_sem)
+    gs_copy.start()
     for copy in adjoint_copies:
         copy.wait()
     for level in range(levels):
         adj_out[1, level] = halo_tile(a_recv[0, level // 2], a_recv[1, level // 2], level % 2)
+
+    def step(i, carry):
+        span = pl.ds(i * BATCH, BATCH)
+        for level in range(levels):
+            own = perturb[span, level].astype(jnp.float32) * adj_out[0, level]
+            halo = ph_out[span, level] * adj_out[1, level]
+            own, halo = diffuse(
+                own, halo, fx_out[0, level], fx_out[1, level], fy_out[0, level], fy_out[1, level]
+            )
+            tail[span, level] = alpha[span, level] + scale * own
+        pltpu.make_async_copy(tail.at[span], ga.at[span], ga_sem.at[i]).start()
+        return carry
+
+    lax.fori_loop(0, members // BATCH, step, 0)
+    for i in range(members // BATCH):
+        span = pl.ds(i * BATCH, BATCH)
+        pltpu.make_async_copy(tail.at[span], ga.at[span], ga_sem.at[i]).wait()
+    gs_copy.wait()
 
 
 def halo_tile(first, second, i):
@@ -257,21 +303,6 @@
     if i == 0:
         return jnp.where(top, first, roll(second, 4, -2))
     return jnp.where(top, roll(first, 4, -2), second)
-
-
-def finish(scale, alpha, perturb, ph, adj, fx, fy, static, sigma, ga, gs):
-    @pl.when(pl.program_id(0) == 0)
-    def _():
-        gs[...] = static[...] + sigma[...] * adj[0]
-
-    for m in range(alpha.shape[0]):
-        for level in range(alpha.shape[1]):
-            own = perturb[m, level].astype(jnp.float32) * adj[0, level]
-            halo = ph[m, level] * adj[1, level]
-            own, halo = diffuse(
-                own, halo, fx[0, level], fx[1, level], fy[0, level], fy[1, level]
-            )
-            ga[m, level] = alpha[m, level] + scale * own
 
 
 def per_device(
@@ -285,19 +316,31 @@
     f32 = jnp.float32
     tile = (levels, columns, rows)
     half = (2, levels // 2, columns, rows)
-    vmem = pl.BlockSpec(memory_space=pltpu.VMEM)
+    hbm = pl.BlockSpec(memory_space=pltpu.HBM)
     dma = pltpu.SemaphoreType.DMA
-    adj, ph, fx, fy = pl.pallas_call(
+    return pl.pallas_call(
         functools.partial(exchange, n_dom, n_ens, scale),
         out_shape=(
-            jax.ShapeDtypeStruct((2,) + tile, f32),
-            jax.ShapeDtypeStruct((local,) + tile, f32),
-            jax.ShapeDtypeStruct((2,) + tile, f32),
-            jax.ShapeDtypeStruct((2,) + tile, f32),
+            jax.ShapeDtypeStruct(alpha.shape, f32),
+            jax.ShapeDtypeStruct(tile, f32),
         ),
-        in_specs=[pl.BlockSpec(memory_space=pltpu.SMEM)] + [vmem] * 8,
-        out_specs=(vmem,) * 4,
+        in_specs=[hbm] * 9,
+        out_specs=(hbm,) * 2,
         scratch_shapes=[
+            pltpu.VMEM((2,) + tile, f32),
+            pltpu.VMEM(alpha.shape, f32),
+            pltpu.VMEM((2,) + tile, f32),
+            pltpu.VMEM((2,) + tile, f32),
+            pltpu.VMEM(alpha.shape, f32),
+            pltpu.VMEM(perturb.shape, perturb.dtype),
+            pltpu.VMEM(tile, f32),
+            pltpu.SMEM(class_kappa.shape, f32),
+            pltpu.VMEM(tile, f32),
+            pltpu.VMEM(tile, f32),
+            pltpu.VMEM(tile, jnp.int32),
+            pltpu.VMEM((groups, LANES), jnp.int32),
+            pltpu.VMEM((groups, LANES), f32),
+            pltpu.VMEM((groups, LANES), f32),
             pltpu.VMEM(half, f32),
             pltpu.VMEM(half, f32),
             pltpu.VMEM((2, local) + half[1:], f32),
@@ -311,6 +354,7 @@
             pltpu.VMEM((2,) + tile, f32),
             pltpu.VMEM((LANES, groups * LANES), jnp.bfloat16),
             pltpu.VMEM((2 * PIECES * LANES, groups * LANES), jnp.bfloat16),
+            dma((8,)), dma((CHUNKS,)), dma((local // BATCH,)), dma(()),
             dma((2,)), dma((2,)),
             dma((2, CHUNKS)), dma((2, CHUNKS)),
             dma((2,)), dma((2,)),
@@ -318,7 +362,7 @@
             dma((n_ens,)), dma((n_ens,)),
         ],
         compiler_params=pltpu.CompilerParams(
-            collective_id=0, has_side_effects=True, vmem_limit_bytes=40 * 2**20
+            collective_id=0, has_side_effects=True, vmem_limit_bytes=60 * 2**20
         ),
         name="exchange",
     )(
@@ -326,22 +370,6 @@
         obs_cell.reshape(groups, LANES), obs_value.reshape(groups, LANES),
         obs_weight.reshape(groups, LANES),
     )
-    block = 2
-    moving = pl.BlockSpec((block,) + tile, lambda i: (i, 0, 0, 0))
-    fixed = pl.BlockSpec((2,) + tile, lambda i: (0, 0, 0, 0))
-    plain = pl.BlockSpec(tile, lambda i: (0, 0, 0))
-    return pl.pallas_call(
-        functools.partial(finish, scale),
-        out_shape=(
-            jax.ShapeDtypeStruct(alpha.shape, f32),
-            jax.ShapeDtypeStruct(static_ctl.shape, f32),
-        ),
-        grid=(local // block,),
-        in_specs=[moving, moving, moving, fixed, fixed, fixed, plain, plain],
-        out_specs=(moving, plain),
-        name="finish",
-    )(alpha, perturb, ph, adj, fx, fy, static_ctl, sigma)
-
 
 def solution(mesh):
     return jax.shard_map(

time: 56 us -> 46.3 us (0.83)
  local copies, waits for them, and re-layouts: 10.1 us -> 2.63 us
  Pallas kernels: 44.6 us -> 42.9 us
    unnamed x26 -> x4, local copies, waits for them, and re-layouts: 10.1 us -> 2.63 us
    pallas_call x1 -> x0, Pallas kernels: 6.63 us -> none  [per_device(): pl.pallas_call(functools.partial(finish, scale), out_shape=(jax.ShapeDtyp...]
    pallas_call x1, Pallas kernels: 38 us -> 42.9 us  [per_device(): pl.pallas_call(functools.partial(exchange, n_dom, n_ens, scale), out_shap...]
where the time goes in v2:
time: 46.3 us; the launch traced here: 46.2 us
  Pallas kernels  42.9 us (93%)
  local copies, waits for them, and re-layouts  2.63 us (6%)
  between operations  0.65 us (1%)
    pallas_call x1, Pallas kernels, per_device(): pl.pallas_call(functools.partial(exchange, n_dom, n_ens, scale), out_shap...  42.9 us
    unnamed x4, local copies, waits for them, and re-layouts  2.63 us

profile of v2, /device:TPU:0, one launch (start us, length us, event | category | flops | bytes accessed | tf_op | source)
XLA Modules:
  0.0 46.2 jit_solution(1239929757225535769)
XLA Ops:
  0.6 42.9 %exchange.1 = (f32[10,4,8,512]{3,2,1,0:T(8,128)}, f32[4,8,512]{2,1,0:T(8,128)}) custom-call(f32[8]{0:T(128)} %kappa_in.1, f32[10,4,8,512]{3,2,1,0:T(8,128)} %alpha_in.1, bf16[10,4,8,512]{3,2,1,0:T(8,128)(2,1)} %perturb_in.1, f32[4,8,512]{2,1,0:T(8,128)} %static_in.1, f32[4,8,512]{2,1,0:T(8,128)} %sigma_in.1, s32[4,8,512]{2,1,0:T(8,128)} %index_in.1, ...), custom_call_target="tpu_custom_call" | custom-call | tf_op jit(solution)/shard_map/exchange/pallas_call | solution.py:321
  43.5 0.0 copy-start
  43.5 2.0 %copy.13 = f32[10,4,8,512]{3,2,1,0:T(8,128)} copy(f32[10,4,8,512]{3,2,1,0:T(8,128)} %get-tuple-element.4) | data formatting | bytes 1310720
  45.5 0.0 copy-done
  45.5 0.6 %copy.14 = f32[4,8,512]{2,1,0:T(8,128)} copy(f32[4,8,512]{2,1,0:T(8,128)S(1)} %copy-done) | data formatting | bytes 131072
Async XLA Ops:
  43.5 2.0 %copy-start = (f32[4,8,512]{2,1,0:T(8,128)S(1)}, f32[4,8,512]{2,1,0:T(8,128)}, u32[]{:S(2)}) copy-start(f32[4,8,512]{2,1,0:T(8,128)} %get-tuple-element.5) | copy-start | bytes 196612

commit v3 on v2

--- a/solution.py
+++ b/solution.py
@@ -203,18 +203,21 @@
             fx_out[0, level], fx_out[1, level], fy_out[0, level], fy_out[1, level] = f
 
     loads[7].wait()
-    for level in range(levels):
-        f = (fx_out[0, level], fx_out[1, level], fy_out[0, level], fy_out[1, level])
-
-        def smooth(i, acc):
-            span = pl.ds(i * BATCH, BATCH)
-            own, halo = diffuse(alpha[span, level], jnp.zeros((BATCH, 8, rows), jnp.float32), *f)
+    def smooth(i, acc):
+        span = pl.ds(i * BATCH, BATCH)
+        for level in range(levels):
+            own, halo = diffuse(
+                alpha[span, level], jnp.zeros((BATCH, 8, rows), jnp.float32),
+                fx_out[0, level], fx_out[1, level], fy_out[0, level], fy_out[1, level],
+            )
             tail[span, level] = halo
-            return acc + jnp.sum(perturb[span, level].astype(jnp.float32) * own, axis=0)
-
-        total[0, level] = lax.fori_loop(
-            0, members // BATCH, smooth, jnp.zeros((8, rows), jnp.float32)
-        )
+            total[0, level] = total[0, level] + jnp.sum(
+                perturb[span, level].astype(jnp.float32) * own, axis=0
+            )
+        return acc
+
+    total[0] = jnp.zeros(total.shape[1:], jnp.float32)
+    lax.fori_loop(0, members // BATCH, smooth, 0)
 
     edge = [jnp.zeros((8, rows), jnp.float32)] * levels
     for chunk in range(CHUNKS):

time: 46.3 us -> 39.9 us (0.86)
  Pallas kernels: 42.9 us -> 36.4 us
    pallas_call x1, Pallas kernels: 42.9 us -> 36.4 us  [per_device(): pl.pallas_call(functools.partial(exchange, n_dom, n_ens, scale), out_shap...]
where the time goes in v3:
time: 39.9 us; the launch traced here: 39.7 us
  Pallas kernels  36.4 us (91%)
  local copies, waits for them, and re-layouts  2.63 us (7%)
  between operations  0.65 us (2%)
    pallas_call x1, Pallas kernels, per_device(): pl.pallas_call(functools.partial(exchange, n_dom, n_ens, scale), out_shap...  36.4 us
    unnamed x4, local copies, waits for them, and re-layouts  2.63 us

profile of v3, /device:TPU:0, one launch (start us, length us, event | category | flops | bytes accessed | tf_op | source)
XLA Modules:
  0.0 39.7 jit_solution(4434171585606725003)
XLA Ops:
  0.6 36.4 %exchange.1 = (f32[10,4,8,512]{3,2,1,0:T(8,128)}, f32[4,8,512]{2,1,0:T(8,128)}) custom-call(f32[8]{0:T(128)} %kappa_in.1, f32[10,4,8,512]{3,2,1,0:T(8,128)} %alpha_in.1, bf16[10,4,8,512]{3,2,1,0:T(8,128)(2,1)} %perturb_in.1, f32[4,8,512]{2,1,0:T(8,128)} %static_in.1, f32[4,8,512]{2,1,0:T(8,128)} %sigma_in.1, s32[4,8,512]{2,1,0:T(8,128)} %index_in.1, ...), custom_call_target="tpu_custom_call" | custom-call | tf_op jit(solution)/shard_map/exchange/pallas_call | solution.py:324
  37.1 0.0 copy-start
  37.1 2.0 %copy.13 = f32[10,4,8,512]{3,2,1,0:T(8,128)} copy(f32[10,4,8,512]{3,2,1,0:T(8,128)} %get-tuple-element.4) | data formatting | bytes 1310720
  39.1 0.0 copy-done
  39.1 0.6 %copy.14 = f32[4,8,512]{2,1,0:T(8,128)} copy(f32[4,8,512]{2,1,0:T(8,128)S(1)} %copy-done) | data formatting | bytes 131072
Async XLA Ops:
  37.1 2.0 %copy-start = (f32[4,8,512]{2,1,0:T(8,128)S(1)}, f32[4,8,512]{2,1,0:T(8,128)}, u32[]{:S(2)}) copy-start(f32[4,8,512]{2,1,0:T(8,128)} %get-tuple-element.5) | copy-start | bytes 196612

commit v4 on v3

--- a/solution.py
+++ b/solution.py
@@ -120,7 +120,7 @@
         )
         for c in range(CHUNKS)
     ]
-    for copy in loads[:2] + perturb_loads + loads[2:]:
+    for copy in perturb_loads[:1] + loads[:2] + perturb_loads[1:] + loads[2:]:
         copy.start()
 
     barrier = pltpu.get_barrier_semaphore()
@@ -139,6 +139,31 @@
         copy.start()
         return copy
 
+    halo_copies = []
+
+    def push(chunk):
+        perturb_loads[chunk].wait()
+
+        def fill(m, carry):
+            for pair in range(levels // 2):
+                a = perturb[m, 2 * pair].astype(jnp.float32)
+                b = perturb[m, 2 * pair + 1].astype(jnp.float32)
+                low, high = pack(a, b)
+                p_send[0, m, pair] = low
+                p_send[1, m, pair] = high
+            return carry
+
+        lax.fori_loop(chunk * part, (chunk + 1) * part, fill, 0, unroll=True)
+        span = pl.ds(chunk * part, part)
+        if chunk == 0:
+            pl.semaphore_wait(barrier, 2 + n_ens - 1)
+        halo_copies.append([
+            send(p_send.at[s, span], p_recv.at[s, span],
+                 p_ss.at[s, chunk], p_rs.at[s, chunk], side)
+            for s, side in ((0, left), (1, right))
+        ])
+
+    push(0)
     loads[0].wait()
     loads[1].wait()
     cls = index[...]
@@ -149,31 +174,12 @@
         low, high = pack(coeff[2 * pair], coeff[2 * pair + 1])
         c_send[0, pair] = low
         c_send[1, pair] = high
-    pl.semaphore_wait(barrier, 2 + n_ens - 1)
     coeff_copies = [
         send(c_send.at[s], c_recv.at[s], c_ss.at[s], c_rs.at[s], side)
         for s, side in ((0, left), (1, right))
     ]
-    halo_copies = []
-    for chunk in range(CHUNKS):
-        perturb_loads[chunk].wait()
-
-        def fill(m, carry):
-            for pair in range(levels // 2):
-                a = perturb[m, 2 * pair].astype(jnp.float32)
-                b = perturb[m, 2 * pair + 1].astype(jnp.float32)
-                low, high = pack(a, b)
-                p_send[0, m, pair] = low
-                p_send[1, m, pair] = high
-            return carry
-
-        lax.fori_loop(chunk * part, (chunk + 1) * part, fill, 0)
-        span = pl.ds(chunk * part, part)
-        halo_copies.append([
-            send(p_send.at[s, span], p_recv.at[s, span],
-                 p_ss.at[s, chunk], p_rs.at[s, chunk], side)
-            for s, side in ((0, left), (1, right))
-        ])
+    for chunk in range(1, CHUNKS):
+        push(chunk)
 
     for copy in loads[2:5]:
         copy.wait()
@@ -232,7 +238,7 @@
                 out.append(acc[level] + halo * tail[m, level])
             return tuple(out)
 
-        edge = lax.fori_loop(chunk * part, (chunk + 1) * part, gather, tuple(edge))
+        edge = lax.fori_loop(chunk * part, (chunk + 1) * part, gather, tuple(edge), unroll=True)
     for pair in range(levels // 2):
         low, high = pack(edge[2 * pair], edge[2 * pair + 1])
         e_send[0, pair] = low

time: 39.9 us -> 39.9 us (level)
  no operation moved by 1% of the time
where the time goes in v4:
time: 39.9 us; the launch traced here: 39.7 us
  Pallas kernels  36.4 us (91%)
  local copies, waits for them, and re-layouts  2.63 us (7%)
  between operations  0.65 us (2%)
    pallas_call x1, Pallas kernels, per_device(): pl.pallas_call(functools.partial(exchange, n_dom, n_ens, scale), out_shap...  36.4 us
    unnamed x4, local copies, waits for them, and re-layouts  2.63 us

profile of v4, /device:TPU:0, one launch (start us, length us, event | category | flops | bytes accessed | tf_op | source)
XLA Modules:
  0.0 39.7 jit_solution(16563839926700587976)
XLA Ops:
  0.6 36.4 %exchange.1 = (f32[10,4,8,512]{3,2,1,0:T(8,128)}, f32[4,8,512]{2,1,0:T(8,128)}) custom-call(f32[8]{0:T(128)} %kappa_in.1, f32[10,4,8,512]{3,2,1,0:T(8,128)} %alpha_in.1, bf16[10,4,8,512]{3,2,1,0:T(8,128)(2,1)} %perturb_in.1, f32[4,8,512]{2,1,0:T(8,128)} %static_in.1, f32[4,8,512]{2,1,0:T(8,128)} %sigma_in.1, s32[4,8,512]{2,1,0:T(8,128)} %index_in.1, ...), custom_call_target="tpu_custom_call" | custom-call | tf_op jit(solution)/shard_map/exchange/pallas_call | solution.py:330
  37.1 0.0 copy-start
  37.1 2.0 %copy.13 = f32[10,4,8,512]{3,2,1,0:T(8,128)} copy(f32[10,4,8,512]{3,2,1,0:T(8,128)} %get-tuple-element.4) | data formatting | bytes 1310720
  39.1 0.0 copy-done
  39.1 0.6 %copy.14 = f32[4,8,512]{2,1,0:T(8,128)} copy(f32[4,8,512]{2,1,0:T(8,128)S(1)} %copy-done) | data formatting | bytes 131072
Async XLA Ops:
  37.1 2.0 %copy-start = (f32[4,8,512]{2,1,0:T(8,128)S(1)}, f32[4,8,512]{2,1,0:T(8,128)}, u32[]{:S(2)}) copy-start(f32[4,8,512]{2,1,0:T(8,128)} %get-tuple-element.5) | copy-start | bytes 196612
